TPU v7x, 32 devices: a whole 2x2x4 slice. The times are simulated.
32 devices in a mesh: seq: 8 (over z, x), fsdp: 4 (over y, core).
Axes of the slice: x: 2, y: 2, z: 4, core: 2. Of those that a mesh axis runs over, the one named last changes fastest.
Arguments:
- inputs: bfloat16 [4, 1024, 768], P('fsdp', 'seq'), may hold values from -6 to 6
- cotangent: bfloat16 [4, 1024, 768], P('fsdp', 'seq'), may hold values from -6 to 6
- inproj: bfloat16 [1, 768, 3352], P(None, 'fsdp'), may hold values from -0.21875 to 0.21875
- outproj: bfloat16 [1, 1536, 768], P(None, 'fsdp'), may hold values from -0.15625 to 0.15625
- norm_gain: float32 [1, 768], replicated, may hold values from 0.5 to 2
- gate_gain: float32 [1, 1536], replicated, may hold values from 0.5 to 2
- conv_weight: float32 [1, 4, 1792], replicated, may hold values from -3 to 3
- conv_bias: float32 [1, 1792], replicated, may hold values from -0.5 to 0.5
- step_bias: float32 [1, 24], replicated, may hold values from -5.5 to -4.5
- log_rate: float32 [1, 24], replicated, may hold values from -7 to 1.5
- skip_gain: float32 [1, 24], replicated, may hold values from 0.5 to 2
Outputs:
- output: bfloat16 [4, 1024, 768], P('fsdp', 'seq')
- input_grad: bfloat16 [4, 1024, 768], P('fsdp', 'seq')
- inproj_grad: float32 [1, 768, 3352], P(None, 'fsdp')
- outproj_grad: float32 [1, 1536, 768], P(None, 'fsdp')
- norm_grad: float32 [1, 768], replicated
- gate_grad: float32 [1, 1536], replicated
- kernel_grad: float32 [1, 4, 1792], replicated
- bias_grad: float32 [1, 1792], replicated
- step_grad: float32 [1, 24], replicated
- rate_grad: float32 [1, 24], replicated
- skip_grad: float32 [1, 24], replicated
All inputs are finite; a program needn't handle non-finite values.
Results may differ from a plain program's by a relative error of at most 0.01.
Values may be sent and summed in bfloat16 or wider, within the bound.
A program may use at most 192 MiB of HBM per device.

v0:
```python
import jax
import jax.numpy as jnp
from jax import lax
from jax.sharding import PartitionSpec as P

H = 24
P_SIZE = 64
N = 128
CONV = 4
SPAN = 64
LAYERS = 1
DI = 1536
XBC = 1792
epsilon = 1e-05
highest = lax.Precision.HIGHEST


def passed_along(shard, axis, by):
    length = lax.axis_size(axis)
    pairs = [(i, i + by) for i in range(length) if 0 <= i + by < length]
    return lax.ppermute(shard, axis, pairs)


def prefix(shard, axis, combine, identity):
    length, index = (lax.axis_size(axis), lax.axis_index(axis))
    everything = jax.tree.map(
        lambda part, kind: lax.all_gather(part.astype(kind), axis),
        shard,
        (jnp.bfloat16, jnp.bfloat16),
    )
    start = jax.tree.map(
        lambda part, zero: jnp.broadcast_to(jnp.asarray(zero, part.dtype), part.shape),
        shard,
        identity,
    )

    def prefix_step(k, before):
        reached = k < index
        new = combine(
            before, jax.tree.map(lambda part, own: part[k].astype(own.dtype), everything, shard)
        )
        return jax.tree.map(lambda a, b: jnp.where(reached, a, b), new, before)

    return lax.fori_loop(0, length, prefix_step, start)


def carried_in(shard, axis, combine, identity):
    length, index = (lax.axis_size(axis), lax.axis_index(axis))
    everything = jax.tree.map(
        lambda part, kind: lax.all_gather(part.astype(kind), axis),
        shard,
        jax.tree.map(lambda a: jnp.bfloat16 if a.dtype == jnp.float32 else a.dtype, shard),
    )
    start = jax.tree.map(
        lambda part, zero: jnp.broadcast_to(jnp.asarray(zero, part.dtype), part.shape),
        shard,
        identity,
    )

    def carried_step(k, before):
        at = length - 1 - k
        reached = at > index
        new = combine(
            before, jax.tree.map(lambda part, own: part[at].astype(own.dtype), everything, shard)
        )
        return jax.tree.map(lambda a, b: jnp.where(reached, a, b), new, before)

    return lax.fori_loop(0, length, carried_step, start)


def rms_scale(values, gain):
    return values * lax.rsqrt(jnp.mean(values * values, axis=-1, keepdims=True) + epsilon) * gain


def section_one(projected, rim_rows, conv_weight, conv_bias, step_bias, log_rate):
    tokens = projected.shape[0]
    conv_input = projected[:, DI : DI + XBC]
    step_raw = projected[:, DI + XBC :]
    extended = jnp.concatenate([rim_rows, conv_input], axis=0)
    conv_sum = conv_bias + conv_weight[0] * extended[0:tokens]
    for offset in range(1, CONV):
        conv_sum = conv_sum + conv_weight[offset] * extended[offset : offset + tokens]
    conv_act = jax.nn.silu(conv_sum)
    blocks = tokens // SPAN
    head_input = conv_act[:, :DI].reshape(blocks, SPAN, H, P_SIZE)
    in_coeff = conv_act[:, DI : DI + N].reshape(blocks, SPAN, N)
    out_coeff = conv_act[:, DI + N :].reshape(blocks, SPAN, N)
    step_size = jax.nn.softplus(step_raw + step_bias).reshape(blocks, SPAN, H)
    decays = -jnp.exp(log_rate) * step_size
    inside = jnp.cumsum(decays, axis=1)
    inside_heads = jnp.swapaxes(inside, 1, 2)
    step_heads = jnp.swapaxes(step_size, 1, 2)
    scores = jnp.einsum("ktn,ksn->kts", out_coeff, in_coeff, precision=highest)
    log_gaps = inside_heads[:, :, :, None] - inside_heads[:, :, None, :]
    causal = jnp.arange(SPAN)[:, None] >= jnp.arange(SPAN)[None, :]
    decay_mat = jnp.exp(jnp.where(causal[None, None], log_gaps, -jnp.inf))
    decay_mat = decay_mat * scores[:, None] * step_heads[:, :, None, :]
    inner_out = jnp.einsum("khts,kshp->kthp", decay_mat, head_input, precision=highest)
    last_log = inside[:, -1:, :]
    tail_weight = jnp.exp(last_log - inside) * step_size
    span_state = jnp.einsum(
        "ksh,kshp,ksn->khpn", tail_weight, head_input, in_coeff, precision=highest
    )
    totals = last_log[:, 0, :]

    def carry_step(carry_state, block_item):
        block_total, block_state = block_item
        return (jnp.exp(block_total)[:, None, None] * carry_state + block_state, carry_state)

    final_state, entering = lax.scan(
        carry_step, jnp.zeros((H, P_SIZE, N), jnp.float32), (totals, span_state)
    )
    cross_out = jnp.einsum(
        "kth,ktn,khpn->kthp", jnp.exp(inside), out_coeff, entering, precision=highest
    )
    offsets = jnp.cumsum(totals, axis=0) - totals
    cumulative = (inside + offsets[:, None, :]).reshape(tokens, H)
    ssm_zero = (inner_out + cross_out).reshape(tokens, H, P_SIZE)
    return (
        ssm_zero,
        cumulative,
        out_coeff.reshape(tokens, N),
        head_input.reshape(tokens, H, P_SIZE),
        final_state,
    )


def section_two(
    projected, ssm_zero, cumulative, out_coeff, head_input, state_in, skip_gain, gate_gain
):
    tokens = projected.shape[0]
    gate_part = projected[:, :DI]
    entering = jnp.einsum("tn,hpn->thp", out_coeff, state_in, precision=highest)
    ssm_full = (
        ssm_zero
        + jnp.exp(cumulative)[:, :, None] * entering
        + skip_gain[None, :, None] * head_input
    )
    gated = ssm_full.reshape(tokens, DI) * jax.nn.silu(gate_part)
    return rms_scale(gated, gate_gain)


def join_states(earlier, later):
    return (earlier[0] + later[0], jnp.exp(later[0])[:, None, None] * earlier[1] + later[1])


def join_grads(earlier, later):
    return (earlier[0] + later[0], later[1] + jnp.exp(later[0])[:, None, None] * earlier[1])


def on_device(
    inputs,
    cotangent,
    inproj,
    outproj,
    norm_gain,
    gate_gain,
    conv_weight,
    conv_bias,
    step_bias,
    log_rate,
    skip_gain,
):
    stream = inputs[0].astype(jnp.float32)
    tokens = stream.shape[0]
    rim_start = tokens - CONV + 1
    layer_index = 0
    inproj_full = lax.all_gather(inproj[layer_index], "fsdp", axis=0, tiled=True)
    outproj_full = lax.all_gather(outproj[layer_index], "fsdp", axis=0, tiled=True)
    normed_f, pull_norm = jax.vjp(rms_scale, stream, norm_gain[layer_index])
    normed = normed_f.astype(jnp.bfloat16)
    projected = jnp.dot(normed, inproj_full, preferred_element_type=jnp.float32)
    rim_rows = passed_along(projected[rim_start:, DI : DI + XBC], "seq", 1)
    first_out, pull_first = jax.vjp(
        section_one,
        projected,
        rim_rows,
        conv_weight[layer_index],
        conv_bias[layer_index],
        step_bias[layer_index],
        log_rate[layer_index],
    )
    ssm_zero, cumulative, out_coeff, head_input, final_state = first_out
    total_log = cumulative[tokens - 1]
    entering = prefix(
        (total_log, final_state),
        "seq",
        join_states,
        (jnp.zeros_like(total_log), jnp.zeros_like(final_state)),
    )
    state_in = entering[1]
    mixed_f, pull_second = jax.vjp(
        section_two,
        projected,
        ssm_zero,
        cumulative,
        out_coeff,
        head_input,
        state_in,
        skip_gain[layer_index],
        gate_gain[layer_index],
    )
    mixed_out = mixed_f.astype(jnp.bfloat16)
    stream = stream + jnp.dot(mixed_out, outproj_full, preferred_element_type=jnp.float32)
    stored = [
        (
            inproj_full,
            outproj_full,
            normed,
            mixed_out,
            pull_norm,
            pull_first,
            pull_second,
            total_log,
            state_in,
        )
    ]
    output = stream.astype(jnp.bfloat16)
    grad_stream = cotangent[0].astype(jnp.float32)
    inproj_list = [None] * LAYERS
    outproj_list = [None] * LAYERS
    small_list = [None] * LAYERS
    contract_rows = (((0,), (0,)), ((), ()))
    for layer_index in reversed(range(LAYERS)):
        (
            inproj_full,
            outproj_full,
            normed,
            mixed_out,
            pull_norm,
            pull_first,
            pull_second,
            total_log,
            state_in,
        ) = stored[layer_index]
        out_grad = grad_stream.astype(jnp.bfloat16)
        mix_grad = jnp.dot(out_grad, outproj_full.T, preferred_element_type=jnp.float32)
        second_grads = pull_second(mix_grad)
        (
            proj_second,
            zero_grad,
            cum_part,
            coeff_grad,
            head_grad,
            state_grad,
            skip_part,
            gate_part,
        ) = second_grads
        later = carried_in(
            (total_log, state_grad),
            "seq",
            join_grads,
            (jnp.zeros_like(total_log), jnp.zeros_like(state_grad)),
        )
        later_grad = later[1]
        total_grad = jnp.sum(later_grad * state_in, axis=(1, 2)) * jnp.exp(total_log)
        cum_grad = cum_part.at[tokens - 1].add(total_grad)
        first_grads = pull_first((zero_grad, cum_grad, coeff_grad, head_grad, later_grad))
        proj_first, rim_grad, kernel_part, bias_part, step_part, rate_part = first_grads
        rim_back = passed_along(rim_grad, "seq", -1)
        proj_grad = (proj_first + proj_second).at[rim_start:, DI : DI + XBC].add(rim_back)
        proj_grad_b = proj_grad.astype(jnp.bfloat16)
        normed_grad = jnp.dot(proj_grad_b, inproj_full.T, preferred_element_type=jnp.float32)
        stream_part, norm_part = pull_norm(normed_grad)
        grad_stream = grad_stream + stream_part
        inproj_term = lax.dot_general(
            normed, proj_grad_b, contract_rows, preferred_element_type=jnp.float32
        )
        outproj_term = lax.dot_general(
            mixed_out, out_grad, contract_rows, preferred_element_type=jnp.float32
        )
        inproj_owned, outproj_owned = (
            lax.psum_scatter(
                inproj_term.astype(jnp.bfloat16), "fsdp", scatter_dimension=0, tiled=True
            ).astype(jnp.float32),
            lax.psum_scatter(
                outproj_term.astype(jnp.bfloat16), "fsdp", scatter_dimension=0, tiled=True
            ).astype(jnp.float32),
        )
        inproj_sum, outproj_sum = lax.psum((inproj_owned, outproj_owned), "seq")
        inproj_list[layer_index] = inproj_sum
        outproj_list[layer_index] = outproj_sum
        small_list[layer_index] = (
            norm_part,
            gate_part,
            kernel_part,
            bias_part,
            step_part,
            rate_part,
            skip_part,
        )
    norm_all, gate_all, kernel_all, bias_all, step_all, rate_all, skip_all = [
        jnp.stack([entry[member] for entry in small_list]) for member in range(7)
    ]
    norm_grad, gate_grad, kernel_grad, bias_grad, step_grad, rate_grad, skip_grad = lax.psum(
        (norm_all, gate_all, kernel_all, bias_all, step_all, rate_all, skip_all), ("seq", "fsdp")
    )
    return (
        output[None],
        grad_stream.astype(jnp.bfloat16)[None],
        jnp.stack(inproj_list),
        jnp.stack(outproj_list),
        norm_grad,
        gate_grad,
        kernel_grad,
        bias_grad,
        step_grad,
        rate_grad,
        skip_grad,
    )


def solution(mesh):
    placed = (
        P("fsdp", "seq", None),
        P("fsdp", "seq", None),
        P(None, "fsdp", None),
        P(None, "fsdp", None),
        P(),
        P(),
        P(),
        P(),
        P(),
        P(),
        P(),
    )
    return jax.shard_map(
        on_device,
        mesh=mesh,
        in_specs=placed,
        out_specs=(
            P("fsdp", "seq", None),
            P("fsdp", "seq", None),
            P(None, "fsdp", None),
            P(None, "fsdp", None),
            P(),
            P(),
            P(),
            P(),
            P(),
            P(),
            P(),
        ),
        check_vma=False,
    )
```

profile of v0, /device:TPU:0, one launch (start us, length us, event | category | flops | bytes accessed | tf_op | source)
XLA Modules:
  0.0 550.7 jit_solution(2837934593614807210)
XLA Ops:
  12.7 40.4 %all-gather.10.cloned.1.call-done = bf16[1,768,3352]{2,1,0:T(8,128)(2,1)} async-done(((bf16[1,192,3352]{2,1,0:T(8,128)(2,1)}), bf16[1,768,3352]{2,1,0:T(8,128)(2,1)}) %all-gather.10.cloned.1.call-update) | async-done | bytes 5148688 | tf_op jit(solution)/shard_map/all_gather | solution.py:168
  53.1 4.7 fusion.8
  61.1 3.5 collective-permute-start
  67.7 5.5 fusion.74
  74.8 2.0 reshape.345
  76.8 2.5 copy.376
  79.3 5.0 fusion.37
  84.5 4.3 while.68
  99.8 21.7 %all-gather.4 = bf16[8,1,24]{2,1,0:T(2,128)(2,1)S(1)} all-gather(bf16[1,1,24]{2,1,0:T(2,128)(2,1)} %bitcast.264), channel_id=1, replica_groups=mesh['seq'=8,'fsdp'=4] {'seq'}, dimensions={0}, use_global_device_ids=true | all-gather | bytes 432 | tf_op jit(solution)/shard_map/all_gather | solution.py:27
  124.8 2.4 fusion.141
  127.3 3.2 fusion.22
  131.7 1.8 reshape.349
  133.5 17.1 %all-gather.12.cloned.1.call-done = bf16[192,64,128]{2,1,0:T(8,128)(2,1)} async-done(((bf16[24,64,128]{2,1,0:T(8,128)(2,1)}), bf16[192,64,128]{2,1,0:T(8,128)(2,1)}) %all-gather.12.cloned.1.call-update) | async-done | bytes 3145744 | tf_op jit(solution)/shard_map/all_gather | solution.py:27
  150.6 15.3 %while.69 = (s32[]{:T(128)}, f32[24,64,128]{2,1,0:T(8,128)S(1)}, s32[]{:T(128)}, bf16[8,24]{1,0:T(8,128)(2,1)}, bf16[8,24,64,128]{3,2,1,0:T(8,128)(2,1)}, /*index=5*/s32[]{:T(128)}, s32[]{:T(128)}) while((s32[]{:T(128)}, f32[24,64,128]{2,1,0:T(8,128)S(1)}, s32[]{:T(128)}, bf16[8,24]{1,0:T(8,128)(2,1)}, ...), condition=%wide.region_6.7_spmd.clone, body=%wide.region_5.6_spmd.clone.sunk | while | flops 983068 | bytes 1966433 | solution.py:44
  170.3 4.6 all-gather.14.cloned.1.call-done
  174.9 3.3 multiply_reduce_fusion.8
  178.3 2.2 multiply_reduce_fusion.7
  183.4 2.2 reshape.353
  185.6 2.1 copy.399
  187.7 3.4 fusion.59
  191.1 2.8 fusion.65
  194.0 4.2 fusion.69
  202.7 2.8 fusion.20
  205.5 2.2 convolution_convert_fusion.1
  208.2 35.0 %all-gather.16.cloned.1.call-done = bf16[192,64,128]{2,1,0:T(8,128)(2,1)} async-done(((bf16[24,64,128]{2,1,0:T(8,128)(2,1)}), bf16[192,64,128]{2,1,0:T(8,128)(2,1)}) %all-gather.16.cloned.1.call-update) | async-done | bytes 3145744 | tf_op jit(solution)/shard_map/all_gather | solution.py:50
  243.2 15.4 %while.70 = (s32[]{:T(128)}, f32[24,64,128]{2,1,0:T(8,128)S(1)}, s32[]{:T(128)}, bf16[8,24,64,128]{3,2,1,0:T(8,128)(2,1)}, bf16[8,24]{1,0:T(8,128)(2,1)}, /*index=5*/s32[]{:T(128)}, s32[]{:T(128)}, s32[]{:T(128)}, s32[]{:T(128)}) while((s32[]{:T(128)}, f32[24,64,128]{2,1,0:T(8,128)S(1)}, s32[]{:T(128)}, ...), condition=%wide.region_10.11_spmd.clone, body=%wide.region_9.10_spmd.clone.sunk | while | flops 983072 | bytes 1966495 | solution.py:68
  262.1 6.6 %while.67 = (s32[]{:T(128)}, f32[24,64,128]{2,1,0:T(8,128)S(1)}, f32[2,24]{1,0:T(2,128)S(1)}, f32[2,24,64,128]{3,2,1,0:T(8,128)}, f32[2,24,64,128]{3,2,1,0:T(8,1...) while((s32[]{:T(128)}, f32[24,64,128]{2,1,0:T(8,128)S(1)}, ...), condition=%wide.region_13.14_spmd, body=%wide.region_11.13_spmd.sunk | while | flops 786435 | bytes 11011073 | solution.py:110
  269.2 3.9 fusion.56
  273.2 4.6 fusion.142
  277.9 4.8 bitcast_add_fusion.2
  283.6 3.8 copy.420
  287.4 2.1 copy.406
  289.5 2.5 reshape.358
  293.5 6.2 %multiply_reduce_fusion.5 = (f32[1792]{0:T(1024)}, f32[1792]{0:T(1024)}, f32[1792]{0:T(1024)}, f32[1792]{0:T(1024)}, f32[1792]{0:T(1024)}, /*index=5*/f32[128,1792]{0,1:T(8,128)S(1)}) fusion(f32[128,1792]{0,1:T(8,128)} %slice.113, f32[3,1792]{0,1:T(8,128)} %copy.364, f32[128,3352]{0,1:T(8,128)S(1)} %copy-done.10, f32[128,1792]{0,1:T(8,128)} %get-tuple-element.620, ...), kind=kLoop, calls=%fused_computation.93 | loop fusion | flops 5266688 | bytes 4644864 | tf_op jit(solution)/shard_map/transpose(jvp())/reduce_sum | solution.py:82
  305.7 3.1 multiply_reduce_fusion
  310.9 2.1 copy.407
  316.3 2.7 collective-permute-done.1
  319.0 2.0 copy.408
  322.5 8.7 %scatter-add.9 = f32[128,3352]{0,1:T(8,128)S(1)} dynamic-update-slice(f32[128,3352]{0,1:T(8,128)S(1)} %pad_add_fusion.1, f32[3,1792]{0,1:T(8,128)S(1)} %slice_add_fusion, s32[]{:T(128)} %constant.233.clone.1, s32[]{:T(128)} %constant.234.clone.1) | dynamic-update-slice | bytes 43012 | tf_op jit(solution)/shard_map/scatter-add | solution.py:261
  331.3 4.0 convolution_convert_fusion
  335.4 2.2 bitcast_convert_fusion.1
  337.5 49.3 %reduce-scatter.3.cloned.1.call-done = bf16[192,3352]{1,0:T(8,128)(2,1)} async-done(((bf16[768,3352]{1,0:T(8,128)(2,1)}), bf16[192,3352]{1,0:T(8,128)(2,1)}) %reduce-scatter.3.cloned.1.call-update) | async-done | bytes 1287184 | tf_op jit(solution)/shard_map/reduce_scatter | solution.py:273
  386.8 3.0 bitcast_convert_fusion
  391.1 3.1 fusion.53
  394.4 4.8 fusion.102
  399.2 44.4 %all-reduce.15 = (f32[1,768]{1,0:T(1,128)}, f32[1,1536]{1,0:T(1,128)}, f32[1,4,1792]{2,1,0:T(4,128)}, f32[1,1792]{1,0:T(1,128)}, f32[1,24]{1,0:T(1,128)}, /*index=5*/f32[1,24]{1,0:T(1,128)}, f32[1,24]{1,0:T(1,128)}) all-reduce(f32[1,768]{1,0:T(1,128)S(1)} %reshape.359, ...), channel_id=1, replica_groups=mesh['seq'=8,'fsdp'=4] {'seq','fsdp'}, use_global_device_ids=true, to_apply=%region_30.31 | all-reduce | flops 11336 | bytes 90688 | tf_op jit(solution)/shard_map/psum | solution.py:295
  444.5 94.6 %all-reduce.19.cloned.1.call-done = (f32[1,192,3352]{2,1,0:T(8,128)}, f32[1,384,768]{2,1,0:T(8,128)}) async-done(((f32[1,192,3352]{2,1,0:T(8,128)}, f32[1,384,768]{2,1,0:T(8,128)}), (f32[1,192,3352]{2,1,0:T(8,128)}, f32[1,384,768]{2,1,0:T(8,128)})) %all-reduce.19.cloned.1.call-update) | async-done | bytes 3754000 | tf_op jit(solution)/shard_map/psum | solution.py:280
  539.1 3.5 copy.534
  (400 shorter events, 104.5 us)
Async XLA Ops:
  7.2 45.9 %copy-start.21 = (bf16[1,128,768]{2,1,0:T(8,128)(2,1)S(1)}, bf16[1,128,768]{2,1,0:T(8,128)(2,1)}, u32[]{:S(2)}) copy-start(bf16[1,128,768]{2,1,0:T(8,128)(2,1)} %param.23) | copy-start | bytes 589828
  7.2 5.5 copy-start.113
  7.2 45.9 %all-gather.10.cloned.1.call-start = ((), (), s32[]{:S(2)}) async-start(), calls=%async_computation.4 | async-start | bytes 6635520 | tf_op jit(solution)/shard_map/all_gather | solution.py:168
  7.9 142.7 %all-gather.12.cloned.1.call-start = ((), (), s32[]{:S(2)}) async-start(), calls=%async_computation.5 | async-start | bytes 3538944 | tf_op jit(solution)/shard_map/all_gather | solution.py:27
  11.6 56.0 %copy-start.67 = (f32[1792]{0:T(1024)}, f32[1792]{0:T(1024)S(1)}, u32[]{:S(2)}) copy-start(f32[1792]{0:T(1024)S(1)} %get-tuple-element.543) | copy-start | bytes 21508
  12.7 45.1 %copy-start.107 = (f32[128]{0:T(128)}, f32[128]{0:T(128)S(1)}, u32[]{:S(2)}) copy-start(f32[128]{0:T(128)S(1)} %fusion.105) | copy-start | bytes 1540
  12.7 45.3 %copy-start.98 = (f32[24]{0:T(128)}, f32[24]{0:T(128)S(1)}, u32[]{:S(2)}) copy-start(f32[24]{0:T(128)S(1)} %negate_bitcast_fusion) | copy-start | bytes 292
  12.7 45.1 %copy-start.91 = (f32[128]{0:T(128)}, f32[128]{0:T(128)S(1)}, u32[]{:S(2)}) copy-start(f32[128]{0:T(128)S(1)} %fusion.124) | copy-start | bytes 1540
  12.7 45.1 %copy-start.101 = (f32[1,24]{1,0:T(1,128)S(1)}, f32[1,24]{1,0:T(1,128)}, u32[]{:S(2)}) copy-start(f32[1,24]{1,0:T(1,128)} %param.31) | copy-start | bytes 292
  57.8 7.5 %copy-start.8 = (f32[128,3352]{0,1:T(8,128)}, f32[128,3352]{0,1:T(8,128)S(1)}, u32[]{:S(2)}) copy-start(f32[128,3352]{0,1:T(8,128)S(1)} %fusion.8) | copy-start | bytes 5148676
  58.0 6.6 %copy-start.40 = (f32[2,64,24]{1,0,2:T(2,128)}, f32[2,64,24]{1,0,2:T(2,128)S(1)}, u32[]{:S(2)}) copy-start(f32[2,64,24]{1,0,2:T(2,128)S(1)} %reshape.346) | copy-start | bytes 36868
  58.3 8.0 %copy-start.37 = (f32[2,64,24]{2,1,0:T(8,128)}, f32[2,64,24]{2,1,0:T(8,128)S(1)}, u32[]{:S(2)}) copy-start(f32[2,64,24]{2,1,0:T(8,128)S(1)} %reduce_window_sum.46) | copy-start | bytes 36868
  58.4 7.9 %copy-start.42 = (f32[2,64,24]{1,2,0:T(8,128)}, f32[2,64,24]{1,2,0:T(8,128)S(1)}, u32[]{:S(2)}) copy-start(f32[2,64,24]{1,2,0:T(8,128)S(1)} %copy.373) | copy-start | bytes 36868
  61.1 6.5 %copy-start.69 = (f32[1792]{0:T(1024)S(1)}, f32[1792]{0:T(1024)}, u32[]{:S(2)}) copy-start(f32[1792]{0:T(1024)} %get-tuple-element.544) | copy-start | bytes 21508
  61.1 6.5 %copy-start.71 = (f32[1792]{0:T(1024)S(1)}, f32[1792]{0:T(1024)}, u32[]{:S(2)}) copy-start(f32[1792]{0:T(1024)} %get-tuple-element.545) | copy-start | bytes 21508
  61.1 6.5 %copy-start.73 = (f32[1792]{0:T(1024)S(1)}, f32[1792]{0:T(1024)}, u32[]{:S(2)}) copy-start(f32[1792]{0:T(1024)} %get-tuple-element.546) | copy-start | bytes 21508
  61.1 6.5 %copy-start.87 = (f32[1792]{0:T(1024)S(1)}, f32[1792]{0:T(1024)}, u32[]{:S(2)}) copy-start(f32[1792]{0:T(1024)} %reduce.9) | copy-start | bytes 21508
  61.1 5.2 collective-permute-start
  73.1 92.8 %copy-start.22 = (f32[128,1792]{0,1:T(8,128)}, f32[128,1792]{0,1:T(8,128)S(1)}, u32[]{:S(2)}) copy-start(f32[128,1792]{0,1:T(8,128)S(1)} %get-tuple-element.619) | copy-start | bytes 2752516
  79.3 5.0 copy-start.5
  88.8 6.0 %copy-start.78 = (f32[2,24]{1,0:T(2,128)}, f32[2,24]{1,0:T(2,128)S(1)}, u32[]{:S(2)}) copy-start(f32[2,24]{1,0:T(2,128)S(1)} %get-tuple-element.947) | copy-start | bytes 580
  88.8 6.0 %copy-start.96 = (f32[2,24]{1,0:T(2,128)}, f32[2,24]{1,0:T(2,128)S(1)}, u32[]{:S(2)}) copy-start(f32[2,24]{1,0:T(2,128)S(1)} %get-tuple-element.879) | copy-start | bytes 580
  88.8 38.4 %copy-start = (f32[2,24,64,128]{3,2,1,0:T(8,128)}, f32[2,24,64,128]{3,2,1,0:T(8,128)S(1)}, u32[]{:S(2)}) copy-start(f32[2,24,64,128]{3,2,1,0:T(8,128)S(1)} %get-tuple-element.878) | copy-start | bytes 4718596
  89.7 85.2 %all-gather.14.cloned.1.call-start = ((), (), s32[]{:S(2)}) async-start(), calls=%async_computation.6 | async-start | bytes 2949120 | tf_op jit(solution)/shard_map/all_gather | solution.py:169
  90.5 152.8 %all-gather.16.cloned.1.call-start = ((), (), s32[]{:S(2)}) async-start(), calls=%async_computation.7 | async-start | bytes 3538944 | tf_op jit(solution)/shard_map/all_gather | solution.py:50
  95.6 31.5 %copy-start.54 = (f32[128,24]{0,1:T(8,128)}, f32[128,24]{0,1:T(8,128)S(1)}, u32[]{:S(2)}) copy-start(f32[128,24]{0,1:T(8,128)S(1)} %copy.379) | copy-start | bytes 36868
  169.3 8.9 %copy-start.11 = (f32[128,1536]{0,1:T(8,128)}, f32[128,1536]{0,1:T(8,128)S(1)}, u32[]{:S(2)}) copy-start(f32[128,1536]{0,1:T(8,128)S(1)} %get-tuple-element.618) | copy-start | bytes 2359300
  183.0 152.3 %reduce-scatter.5.cloned.1.call-start = ((), (), s32[]{:S(2)}) async-start(), calls=%async_computation.3 | async-start | bytes 2949120 | tf_op jit(solution)/shard_map/reduce_scatter | solution.py:276
  207.7 179.1 %reduce-scatter.3.cloned.1.call-start = ((), (), s32[]{:S(2)}) async-start(), calls=%async_computation.2 | async-start | bytes 6635520 | tf_op jit(solution)/shard_map/reduce_scatter | solution.py:273
  262.1 7.2 %copy-start.47 = (f32[2,64,24]{1,2,0:T(8,128)S(1)}, f32[2,64,24]{1,2,0:T(8,128)}, u32[]{:S(2)}) copy-start(f32[2,64,24]{1,2,0:T(8,128)} %get-tuple-element.631) | copy-start | bytes 36868
  273.2 4.7 copy-start.15
  273.2 4.7 copy-start.46
  277.9 4.8 copy-start.18
  277.9 4.8 copy-start.53
  293.5 6.3 %copy-start.68 = (f32[1792]{0:T(1024)S(1)}, f32[1792]{0:T(1024)}, u32[]{:S(2)}) copy-start(f32[1792]{0:T(1024)} %copy-done.67) | copy-start | bytes 21508
  293.5 6.3 %copy-start.70 = (f32[1792]{0:T(1024)S(1)}, f32[1792]{0:T(1024)}, u32[]{:S(2)}) copy-start(f32[1792]{0:T(1024)} %get-tuple-element.544) | copy-start | bytes 21508
  293.5 6.3 %copy-start.72 = (f32[1792]{0:T(1024)S(1)}, f32[1792]{0:T(1024)}, u32[]{:S(2)}) copy-start(f32[1792]{0:T(1024)} %get-tuple-element.545) | copy-start | bytes 21508
  293.5 6.3 %copy-start.74 = (f32[1792]{0:T(1024)S(1)}, f32[1792]{0:T(1024)}, u32[]{:S(2)}) copy-start(f32[1792]{0:T(1024)} %get-tuple-element.546) | copy-start | bytes 21508
  305.7 4.9 copy-start.90
  305.7 4.9 copy-start.99
  308.8 5.4 copy-start.102
  308.9 6.1 %copy-start.31 = (f32[128,1536]{0,1:T(8,128)S(1)}, f32[128,1536]{0,1:T(8,128)}, u32[]{:S(2)}) copy-start(f32[128,1536]{0,1:T(8,128)} %get-tuple-element.623) | copy-start | bytes 2359300
  312.9 6.1 %collective-permute-start.1 = (f32[3,1792]{1,0:T(4,128)}, f32[3,1792]{1,0:T(4,128)}, u32[]{:S(2)}, u32[]{:S(2)}) collective-permute-start(f32[3,1792]{1,0:T(4,128)} %copy.407), channel_id=1, source_target_pairs={{4,0},{8,4},{12,8},{16,12},{20,16},{24,20},{28,24},{5,1},{9,5},{13... | collective-permute-start | bytes 64520 | tf_op jit(solution)/shard_map/ppermute | solution.py:21
  322.5 8.7 %copy-start.92 = (f32[128]{0:T(128)S(1)}, f32[128]{0:T(128)}, u32[]{:S(2)}) copy-start(f32[128]{0:T(128)} %copy-done.91) | copy-start | bytes 1540
  335.3 203.8 %all-reduce.19.cloned.1.call-start = ((), (), s32[]{:S(2)}) async-start(), calls=%async_computation.8 | async-start | bytes 7667712 | tf_op jit(solution)/shard_map/psum | solution.py:280
  394.4 4.8 copy-start.100
  394.4 49.2 %copy-start.108 = (f32[128]{0:T(128)S(1)}, f32[128]{0:T(128)}, u32[]{:S(2)}) copy-start(f32[128]{0:T(128)} %copy-done.107) | copy-start | bytes 1540
  394.4 49.2 %copy-start.34 = (bf16[1,128,768]{2,1,0:T(8,128)(2,1)S(1)}, bf16[1,128,768]{2,1,0:T(8,128)(2,1)}, u32[]{:S(2)}) copy-start(bf16[1,128,768]{2,1,0:T(8,128)(2,1)} %param.24) | copy-start | bytes 589828
  (78 other events, 196.5 us)
Sparse Core Ops, SparseCore 0:
  9.6 43.4 all-gather.9
  89.8 60.7 all-gather.11
  152.2 22.6 all-gather.13
  183.1 60.0 all-gather.15
  246.2 31.4 reduce-scatter.4
  335.4 51.3 reduce-scatter.2
  391.1 147.9 all-reduce.18
where the time goes:
time: 560 us; the launch traced here: 551 us
  waiting for transfers between devices  245 us (44%)
  other arithmetic  78.2 us (14%)
  local copies, waits for them, and re-layouts  75.6 us (13%)
  blocking collectives  66.1 us (12%)
  matrix products  63.5 us (11%)
  between operations  15.7 us (3%)
  starting transfers between devices  5.68 us (1%)
    psum x1, waiting for transfers between devices, on_device(): inproj_sum, outproj_sum = lax.psum((inproj_owned, outproj_owned), 'seq')  94.6 us
    reduce_scatter x1, waiting for transfers between devices, on_device(): lax.psum_scatter(inproj_term.astype(jnp.bfloat16), 'fsdp', scatter_dimens...  49.3 us
    psum x1, blocking collectives, on_device(): lax.psum((norm_all, gate_all, kernel_all, bias_all, step_all, rate_all, s...  44.4 us
    all_gather x1, waiting for transfers between devices, on_device(): lax.all_gather(inproj[layer_index], 'fsdp', axis=0, tiled=True)  40.4 us
    all_gather x1, waiting for transfers between devices, carried_in(): lax.all_gather(part.astype(kind), axis)  35 us
    all_gather x1, blocking collectives, prefix(): lax.all_gather(part.astype(kind), axis)  21.7 us
    unnamed x231, local copies, waits for them, and re-layouts  17.7 us
    all_gather x1, waiting for transfers between devices, prefix(): lax.all_gather(part.astype(kind), axis)  17.1 us
  transfers between devices with their start and end apart: 9, of which 7 were waited for; matrix products, arithmetic and copies ran while one was open for 30% of the time, Pallas kernels for 0%

commit v1 on v0

--- a/solution.py
+++ b/solution.py
@@ -165,7 +165,12 @@
     tokens = stream.shape[0]
     rim_start = tokens - CONV + 1
     layer_index = 0
-    inproj_full = lax.all_gather(inproj[layer_index], "fsdp", axis=0, tiled=True)
+    ring = [inproj[layer_index]]
+    for hop in range(3):
+        ring.append(lax.ppermute(ring[-1], "fsdp", [(dev, (dev + 1) % 4) for dev in range(4)]))
+    inproj_full = jnp.roll(
+        jnp.concatenate(ring[::-1], axis=0), (lax.axis_index("fsdp") + 1) * ring[0].shape[0], axis=0
+    )
     outproj_full = lax.all_gather(outproj[layer_index], "fsdp", axis=0, tiled=True)
     normed_f, pull_norm = jax.vjp(rms_scale, stream, norm_gain[layer_index])
     normed = normed_f.astype(jnp.bfloat16)

time: 560 us -> 578 us (1.032)
  local copies, waits for them, and re-layouts: 75.6 us -> 84.9 us
  waiting for transfers between devices: 245 us -> 252 us
    ppermute x0 -> x3, waiting for transfers between devices: none -> 46.7 us  [on_device(): lax.ppermute(ring[-1], 'fsdp', [(dev, (dev + 1) % 4) for dev in range(4)])]
    all_gather x1 -> x0, waiting for transfers between devices: 40.4 us -> none  [on_device(): lax.all_gather(inproj[layer_index], 'fsdp', axis=0, tiled=True)]
    unnamed x231 -> x244, local copies, waits for them, and re-layouts: 17.7 us -> 26.8 us
  transfers between devices with their start and end apart: 9 -> 11, of which waited for: 7 -> 9; matrix products, arithmetic and copies ran while one was open for 30% -> 29% of each run, Pallas kernels for 0% -> 0%
where the time goes in v1:
time: 578 us; the launch traced here: 567 us
  waiting for transfers between devices  252 us (44%)
  local copies, waits for them, and re-layouts  84.9 us (15%)
  other arithmetic  79 us (14%)
  blocking collectives  65.9 us (11%)
  matrix products  61.4 us (11%)
  between operations  15.8 us (3%)
  starting transfers between devices  7.1 us (1%)
    psum x1, waiting for transfers between devices, on_device(): inproj_sum, outproj_sum = lax.psum((inproj_owned, outproj_owned), 'seq')  94.6 us
    reduce_scatter x1, waiting for transfers between devices, on_device(): lax.psum_scatter(inproj_term.astype(jnp.bfloat16), 'fsdp', scatter_dimens...  49.3 us
    ppermute x3, waiting for transfers between devices, on_device(): lax.ppermute(ring[-1], 'fsdp', [(dev, (dev + 1) % 4) for dev in range(4)])  46.7 us
    psum x1, blocking collectives, on_device(): lax.psum((norm_all, gate_all, kernel_all, bias_all, step_all, rate_all, s...  44 us
    all_gather x1, waiting for transfers between devices, carried_in(): lax.all_gather(part.astype(kind), axis)  35.2 us
    unnamed x244, local copies, waits for them, and re-layouts  26.8 us
    all_gather x1, blocking collectives, prefix(): lax.all_gather(part.astype(kind), axis)  21.9 us
    all_gather x1, waiting for transfers between devices, prefix(): lax.all_gather(part.astype(kind), axis)  18.2 us
  transfers between devices with their start and end apart: 11, of which 9 were waited for; matrix products, arithmetic and copies ran while one was open for 29% of the time, Pallas kernels for 0%

profile of v1, /device:TPU:0, one launch (start us, length us, event | category | flops | bytes accessed | tf_op | source)
XLA Modules:
  0.0 566.7 jit_solution(10062592755605365082)
XLA Ops:
  7.8 17.6 %collective-permute-done = bf16[192,3352]{1,0:T(8,128)(2,1)S(1)} collective-permute-done((bf16[192,3352]{1,0:T(8,128)(2,1)}, bf16[192,3352]{1,0:T(8,128)(2,1)S(1)}, u32[]{:S(2)}, u32[]{:S(2)}) %collective-permute-start) | collective-permute-done | bytes 1287200 | tf_op jit(solution)/shard_map/ppermute | solution.py:170
  25.4 17.2 %collective-permute-done.1 = bf16[192,3352]{1,0:T(8,128)(2,1)S(1)} collective-permute-done((bf16[192,3352]{1,0:T(8,128)(2,1)S(1)}, bf16[192,3352]{1,0:T(8,128)(2,1)S(1)}, u32[]{:S(2)}, u32[]{:S(2)}) %collective-permute-start.1) | collective-permute-done | bytes 1287200 | tf_op jit(solution)/shard_map/ppermute | solution.py:170
  48.0 11.9 %collective-permute-done.2 = bf16[192,3352]{1,0:T(8,128)(2,1)} collective-permute-done((bf16[192,3352]{1,0:T(8,128)(2,1)S(1)}, bf16[192,3352]{1,0:T(8,128)(2,1)}, u32[]{:S(2)}, u32[]{:S(2)}) %collective-permute-start.2) | collective-permute-done | bytes 1287200 | tf_op jit(solution)/shard_map/ppermute | solution.py:170
  65.3 4.0 copy-done.20
  69.4 2.5 fusion.8
  75.2 4.3 collective-permute-start.3
  82.5 5.4 fusion.74
  91.5 2.5 copy.376
  94.1 5.0 fusion.37
  99.2 4.3 while.68
  114.6 21.9 %all-gather.3 = bf16[8,1,24]{2,1,0:T(2,128)(2,1)S(1)} all-gather(bf16[1,1,24]{2,1,0:T(2,128)(2,1)} %bitcast.261), channel_id=1, replica_groups=mesh['seq'=8,'fsdp'=4] {'seq'}, dimensions={0}, use_global_device_ids=true | all-gather | bytes 432 | tf_op jit(solution)/shard_map/all_gather | solution.py:27
  139.8 2.4 fusion.143
  142.3 3.2 fusion.22
  148.4 18.2 %all-gather.8.cloned.1.call-done = bf16[192,64,128]{2,1,0:T(8,128)(2,1)} async-done(((bf16[24,64,128]{2,1,0:T(8,128)(2,1)}), bf16[192,64,128]{2,1,0:T(8,128)(2,1)}) %all-gather.8.cloned.1.call-update) | async-done | bytes 3145744 | tf_op jit(solution)/shard_map/all_gather | solution.py:27
  166.6 15.2 %while.69 = (s32[]{:T(128)}, f32[24,64,128]{2,1,0:T(8,128)S(1)}, s32[]{:T(128)}, bf16[8,24]{1,0:T(8,128)(2,1)}, bf16[8,24,64,128]{3,2,1,0:T(8,128)(2,1)}, /*index=5*/s32[]{:T(128)}, s32[]{:T(128)}) while((s32[]{:T(128)}, f32[24,64,128]{2,1,0:T(8,128)S(1)}, s32[]{:T(128)}, bf16[8,24]{1,0:T(8,128)(2,1)}, ...), condition=%wide.region_6.7_spmd.clone, body=%wide.region_5.6_spmd.clone.sunk | while | flops 983068 | bytes 1966433 | solution.py:44
  186.3 4.6 all-gather.10.cloned.1.call-done
  190.9 3.3 multiply_reduce_fusion.8
  194.3 2.2 multiply_reduce_fusion.7
  199.2 2.2 reshape.353
  201.5 2.1 copy.399
  203.6 3.4 fusion.59
  207.0 2.8 fusion.65
  209.9 4.2 fusion.69
  218.6 2.7 fusion.20
  221.3 2.2 convolution_convert_fusion.1
  224.0 35.2 %all-gather.12.cloned.1.call-done = bf16[192,64,128]{2,1,0:T(8,128)(2,1)} async-done(((bf16[24,64,128]{2,1,0:T(8,128)(2,1)}), bf16[192,64,128]{2,1,0:T(8,128)(2,1)}) %all-gather.12.cloned.1.call-update) | async-done | bytes 3145744 | tf_op jit(solution)/shard_map/all_gather | solution.py:50
  259.2 15.4 %while.70 = (s32[]{:T(128)}, f32[24,64,128]{2,1,0:T(8,128)S(1)}, s32[]{:T(128)}, bf16[8,24,64,128]{3,2,1,0:T(8,128)(2,1)}, bf16[8,24]{1,0:T(8,128)(2,1)}, /*index=5*/s32[]{:T(128)}, s32[]{:T(128)}, s32[]{:T(128)}, s32[]{:T(128)}) while((s32[]{:T(128)}, f32[24,64,128]{2,1,0:T(8,128)S(1)}, s32[]{:T(128)}, ...), condition=%wide.region_10.11_spmd.clone, body=%wide.region_9.10_spmd.clone.sunk | while | flops 983072 | bytes 1966495 | solution.py:68
  278.1 6.6 %while.67 = (s32[]{:T(128)}, f32[24,64,128]{2,1,0:T(8,128)S(1)}, f32[2,24]{1,0:T(2,128)S(1)}, f32[2,24,64,128]{3,2,1,0:T(8,128)}, f32[2,24,64,128]{3,2,1,0:T(8,1...) while((s32[]{:T(128)}, f32[24,64,128]{2,1,0:T(8,128)S(1)}, ...), condition=%wide.region_13.14_spmd, body=%wide.region_11.13_spmd.sunk | while | flops 786435 | bytes 11011073 | solution.py:110
  285.2 3.9 fusion.56
  289.2 4.6 fusion.144
  293.9 4.8 bitcast_add_fusion.2
  299.6 3.8 copy.420
  303.4 2.1 copy.406
  305.5 2.5 reshape.358
  309.6 6.5 %multiply_reduce_fusion.5 = (f32[1792]{0:T(1024)}, f32[1792]{0:T(1024)}, f32[1792]{0:T(1024)}, f32[1792]{0:T(1024)}, f32[1792]{0:T(1024)}, /*index=5*/f32[128,1792]{0,1:T(8,128)S(1)}) fusion(f32[128,1792]{0,1:T(8,128)} %slice.113, f32[3,1792]{0,1:T(8,128)} %copy.364, f32[128,3352]{0,1:T(8,128)S(1)} %copy-done.10, f32[128,1792]{0,1:T(8,128)} %get-tuple-element.620, ...), kind=kLoop, calls=%fused_computation.93 | loop fusion | flops 5266688 | bytes 4644864 | tf_op jit(solution)/shard_map/transpose(jvp())/reduce_sum | solution.py:82
  322.0 3.1 multiply_reduce_fusion
  327.1 2.1 copy.407
  332.5 2.7 collective-permute-done.4
  338.8 8.7 %scatter-add.9 = f32[128,3352]{0,1:T(8,128)S(1)} dynamic-update-slice(f32[128,3352]{0,1:T(8,128)S(1)} %pad_add_fusion.1, f32[3,1792]{0,1:T(8,128)S(1)} %slice_add_fusion, s32[]{:T(128)} %constant.258.clone.1, s32[]{:T(128)} %constant.259.clone.1) | dynamic-update-slice | bytes 43012 | tf_op jit(solution)/shard_map/scatter-add | solution.py:266
  347.5 4.0 convolution_convert_fusion
  351.6 2.2 bitcast_convert_fusion.1
  353.8 49.3 %reduce-scatter.3.cloned.1.call-done = bf16[192,3352]{1,0:T(8,128)(2,1)} async-done(((bf16[768,3352]{1,0:T(8,128)(2,1)}), bf16[192,3352]{1,0:T(8,128)(2,1)}) %reduce-scatter.3.cloned.1.call-update) | async-done | bytes 1287184 | tf_op jit(solution)/shard_map/reduce_scatter | solution.py:278
  403.1 3.0 bitcast_convert_fusion
  407.3 3.1 fusion.53
  410.7 5.0 fusion.102
  415.7 44.0 %all-reduce.15 = (f32[1,768]{1,0:T(1,128)}, f32[1,1536]{1,0:T(1,128)}, f32[1,4,1792]{2,1,0:T(4,128)}, f32[1,1792]{1,0:T(1,128)}, f32[1,24]{1,0:T(1,128)}, /*index=5*/f32[1,24]{1,0:T(1,128)}, f32[1,24]{1,0:T(1,128)}) all-reduce(f32[1,768]{1,0:T(1,128)S(1)} %reshape.359, ...), channel_id=1, replica_groups=mesh['seq'=8,'fsdp'=4] {'seq','fsdp'}, use_global_device_ids=true, to_apply=%region_30.31 | all-reduce | flops 11336 | bytes 90688 | tf_op jit(solution)/shard_map/psum | solution.py:300
  460.5 94.6 %all-reduce.19.cloned.1.call-done = (f32[1,192,3352]{2,1,0:T(8,128)}, f32[1,384,768]{2,1,0:T(8,128)}) async-done(((f32[1,192,3352]{2,1,0:T(8,128)}, f32[1,384,768]{2,1,0:T(8,128)}), (f32[1,192,3352]{2,1,0:T(8,128)}, f32[1,384,768]{2,1,0:T(8,128)})) %all-reduce.19.cloned.1.call-update) | async-done | bytes 3754000 | tf_op jit(solution)/shard_map/psum | solution.py:285
  555.1 3.5 copy.541
  (417 shorter events, 116.2 us)
Async XLA Ops:
  7.2 159.4 %all-gather.8.cloned.1.call-start = ((), (), s32[]{:S(2)}) async-start(), calls=%async_computation.4 | async-start | bytes 3538944 | tf_op jit(solution)/shard_map/all_gather | solution.py:27
  7.2 18.2 %collective-permute-start = (bf16[192,3352]{1,0:T(8,128)(2,1)}, bf16[192,3352]{1,0:T(8,128)(2,1)S(1)}, u32[]{:S(2)}, u32[]{:S(2)}) collective-permute-start(bf16[192,3352]{1,0:T(8,128)(2,1)} %bitcast.234), channel_id=1, source_target_pairs={{0,1},{1,2},{2,3},{3,0},{4,5},{5,6},{6,7},{7,4},{8,9},{9,10},{10,1... | collective-permute-start | bytes 3861512 | tf_op jit(solution)/shard_map/ppermute | solution.py:170
  25.4 17.2 %collective-permute-start.1 = (bf16[192,3352]{1,0:T(8,128)(2,1)S(1)}, bf16[192,3352]{1,0:T(8,128)(2,1)S(1)}, u32[]{:S(2)}, u32[]{:S(2)}) collective-permute-start(bf16[192,3352]{1,0:T(8,128)(2,1)S(1)} %collective-permute-done), channel_id=1, source_target_pairs={{0,1},{1,2},{2,3},{3,0},{4,5},{5,6},{6,7},{7,4},{8,9},{9,10},{10,1... | collective-permute-start | bytes 3861512 | tf_op jit(solution)/shard_map/ppermute | solution.py:170
  42.6 18.7 %copy-start.33 = (bf16[192,3352]{1,0:T(8,128)(2,1)}, bf16[192,3352]{1,0:T(8,128)(2,1)S(1)}, u32[]{:S(2)}) copy-start(bf16[192,3352]{1,0:T(8,128)(2,1)S(1)} %collective-permute-done.1) | copy-start | bytes 3861508
  42.6 17.3 %collective-permute-start.2 = (bf16[192,3352]{1,0:T(8,128)(2,1)S(1)}, bf16[192,3352]{1,0:T(8,128)(2,1)}, u32[]{:S(2)}, u32[]{:S(2)}) collective-permute-start(bf16[192,3352]{1,0:T(8,128)(2,1)S(1)} %collective-permute-done.1), channel_id=1, source_target_pairs={{0,1},{1,2},{2,3},{3,0},{4,5},{5,6},{6,7},{7,4},{8,9},{9,10},{10,1... | collective-permute-start | bytes 3861512 | tf_op jit(solution)/shard_map/ppermute | solution.py:170
  47.3 14.2 %copy-start.111 = (f32[128]{0:T(128)}, f32[128]{0:T(128)S(1)}, u32[]{:S(2)}) copy-start(f32[128]{0:T(128)S(1)} %fusion.105) | copy-start | bytes 1540
  47.9 24.1 %copy-start.102 = (f32[24]{0:T(128)}, f32[24]{0:T(128)S(1)}, u32[]{:S(2)}) copy-start(f32[24]{0:T(128)S(1)} %negate_bitcast_fusion) | copy-start | bytes 292
  48.0 17.3 %copy-start.95 = (f32[128]{0:T(128)}, f32[128]{0:T(128)S(1)}, u32[]{:S(2)}) copy-start(f32[128]{0:T(128)S(1)} %fusion.126) | copy-start | bytes 1540
  71.9 8.3 %copy-start.8 = (f32[128,3352]{0,1:T(8,128)}, f32[128,3352]{0,1:T(8,128)S(1)}, u32[]{:S(2)}) copy-start(f32[128,3352]{0,1:T(8,128)S(1)} %fusion.8) | copy-start | bytes 5148676
  72.1 7.4 %copy-start.44 = (f32[2,64,24]{1,0,2:T(2,128)}, f32[2,64,24]{1,0,2:T(2,128)S(1)}, u32[]{:S(2)}) copy-start(f32[2,64,24]{1,0,2:T(2,128)S(1)} %reshape.346) | copy-start | bytes 36868
  72.3 8.8 %copy-start.41 = (f32[2,64,24]{2,1,0:T(8,128)}, f32[2,64,24]{2,1,0:T(8,128)S(1)}, u32[]{:S(2)}) copy-start(f32[2,64,24]{2,1,0:T(8,128)S(1)} %reduce_window_sum.46) | copy-start | bytes 36868
  72.4 8.7 %copy-start.46 = (f32[2,64,24]{1,2,0:T(8,128)}, f32[2,64,24]{1,2,0:T(8,128)S(1)}, u32[]{:S(2)}) copy-start(f32[2,64,24]{1,2,0:T(8,128)S(1)} %copy.373) | copy-start | bytes 36868
  75.1 7.3 %copy-start.71 = (f32[1792]{0:T(1024)S(1)}, f32[1792]{0:T(1024)}, u32[]{:S(2)}) copy-start(f32[1792]{0:T(1024)} %get-tuple-element.543) | copy-start | bytes 21508
  75.1 7.3 %copy-start.73 = (f32[1792]{0:T(1024)S(1)}, f32[1792]{0:T(1024)}, u32[]{:S(2)}) copy-start(f32[1792]{0:T(1024)} %get-tuple-element.544) | copy-start | bytes 21508
  75.1 7.3 %copy-start.75 = (f32[1792]{0:T(1024)S(1)}, f32[1792]{0:T(1024)}, u32[]{:S(2)}) copy-start(f32[1792]{0:T(1024)} %get-tuple-element.545) | copy-start | bytes 21508
  75.2 7.3 %copy-start.77 = (f32[1792]{0:T(1024)S(1)}, f32[1792]{0:T(1024)}, u32[]{:S(2)}) copy-start(f32[1792]{0:T(1024)} %get-tuple-element.546) | copy-start | bytes 21508
  75.2 7.3 %copy-start.91 = (f32[1792]{0:T(1024)S(1)}, f32[1792]{0:T(1024)}, u32[]{:S(2)}) copy-start(f32[1792]{0:T(1024)} %reduce.9) | copy-start | bytes 21508
  75.2 6.0 %collective-permute-start.3 = (f32[3,1792]{1,0:T(4,128)S(1)}, f32[3,1792]{1,0:T(4,128)S(1)}, u32[]{:S(2)}, u32[]{:S(2)}) collective-permute-start(f32[3,1792]{1,0:T(4,128)S(1)} %copy.363), channel_id=1, source_target_pairs={{0,4},{4,8},{8,12},{12,16},{16,20},{20,24},{24,28},{1,5},{5,9},{9,... | collective-permute-start | bytes 64520 | tf_op jit(solution)/shard_map/ppermute | solution.py:21
  87.8 94.1 %copy-start.23 = (f32[128,1792]{0,1:T(8,128)}, f32[128,1792]{0,1:T(8,128)S(1)}, u32[]{:S(2)}) copy-start(f32[128,1792]{0,1:T(8,128)S(1)} %get-tuple-element.619) | copy-start | bytes 2752516
  94.1 5.0 copy-start.5
  103.5 6.0 %copy-start.82 = (f32[2,24]{1,0:T(2,128)}, f32[2,24]{1,0:T(2,128)S(1)}, u32[]{:S(2)}) copy-start(f32[2,24]{1,0:T(2,128)S(1)} %get-tuple-element.948) | copy-start | bytes 580
  103.5 6.0 %copy-start.100 = (f32[2,24]{1,0:T(2,128)}, f32[2,24]{1,0:T(2,128)S(1)}, u32[]{:S(2)}) copy-start(f32[2,24]{1,0:T(2,128)S(1)} %get-tuple-element.879) | copy-start | bytes 580
  103.5 38.7 %copy-start = (f32[2,24,64,128]{3,2,1,0:T(8,128)}, f32[2,24,64,128]{3,2,1,0:T(8,128)S(1)}, u32[]{:S(2)}) copy-start(f32[2,24,64,128]{3,2,1,0:T(8,128)S(1)} %get-tuple-element.878) | copy-start | bytes 4718596
  104.4 86.5 %all-gather.10.cloned.1.call-start = ((), (), s32[]{:S(2)}) async-start(), calls=%async_computation.5 | async-start | bytes 2949120 | tf_op jit(solution)/shard_map/all_gather | solution.py:174
  105.2 154.0 %all-gather.12.cloned.1.call-start = ((), (), s32[]{:S(2)}) async-start(), calls=%async_computation.6 | async-start | bytes 3538944 | tf_op jit(solution)/shard_map/all_gather | solution.py:50
  110.4 31.8 %copy-start.58 = (f32[128,24]{0,1:T(8,128)}, f32[128,24]{0,1:T(8,128)S(1)}, u32[]{:S(2)}) copy-start(f32[128,24]{0,1:T(8,128)S(1)} %copy.379) | copy-start | bytes 36868
  185.3 8.9 %copy-start.11 = (f32[128,1536]{0,1:T(8,128)}, f32[128,1536]{0,1:T(8,128)S(1)}, u32[]{:S(2)}) copy-start(f32[128,1536]{0,1:T(8,128)S(1)} %get-tuple-element.618) | copy-start | bytes 2359300
  198.9 152.7 %reduce-scatter.5.cloned.1.call-start = ((), (), s32[]{:S(2)}) async-start(), calls=%async_computation.3 | async-start | bytes 2949120 | tf_op jit(solution)/shard_map/reduce_scatter | solution.py:281
  223.5 179.5 %reduce-scatter.3.cloned.1.call-start = ((), (), s32[]{:S(2)}) async-start(), calls=%async_computation.2 | async-start | bytes 6635520 | tf_op jit(solution)/shard_map/reduce_scatter | solution.py:278
  278.1 7.2 %copy-start.51 = (f32[2,64,24]{1,2,0:T(8,128)S(1)}, f32[2,64,24]{1,2,0:T(8,128)}, u32[]{:S(2)}) copy-start(f32[2,64,24]{1,2,0:T(8,128)} %get-tuple-element.631) | copy-start | bytes 36868
  289.2 4.7 copy-start.15
  289.2 4.7 copy-start.50
  293.9 4.8 copy-start.18
  293.9 4.8 copy-start.57
  309.6 6.5 %copy-start.72 = (f32[1792]{0:T(1024)S(1)}, f32[1792]{0:T(1024)}, u32[]{:S(2)}) copy-start(f32[1792]{0:T(1024)} %get-tuple-element.543) | copy-start | bytes 21508
  309.6 6.5 %copy-start.74 = (f32[1792]{0:T(1024)S(1)}, f32[1792]{0:T(1024)}, u32[]{:S(2)}) copy-start(f32[1792]{0:T(1024)} %get-tuple-element.544) | copy-start | bytes 21508
  309.6 6.5 %copy-start.76 = (f32[1792]{0:T(1024)S(1)}, f32[1792]{0:T(1024)}, u32[]{:S(2)}) copy-start(f32[1792]{0:T(1024)} %get-tuple-element.545) | copy-start | bytes 21508
  309.6 6.5 %copy-start.78 = (f32[1792]{0:T(1024)S(1)}, f32[1792]{0:T(1024)}, u32[]{:S(2)}) copy-start(f32[1792]{0:T(1024)} %get-tuple-element.546) | copy-start | bytes 21508
  322.0 4.9 copy-start.94
  322.0 4.9 copy-start.103
  325.1 5.4 copy-start.106
  325.1 6.1 %copy-start.35 = (f32[128,1536]{0,1:T(8,128)S(1)}, f32[128,1536]{0,1:T(8,128)}, u32[]{:S(2)}) copy-start(f32[128,1536]{0,1:T(8,128)} %get-tuple-element.623) | copy-start | bytes 2359300
  329.2 6.1 %collective-permute-start.4 = (f32[3,1792]{1,0:T(4,128)}, f32[3,1792]{1,0:T(4,128)}, u32[]{:S(2)}, u32[]{:S(2)}) collective-permute-start(f32[3,1792]{1,0:T(4,128)} %copy.407), channel_id=1, source_target_pairs={{4,0},{8,4},{12,8},{16,12},{20,16},{24,20},{28,24},{5,1},{9,5},{13... | collective-permute-start | bytes 64520 | tf_op jit(solution)/shard_map/ppermute | solution.py:21
  338.8 8.7 %copy-start.96 = (f32[128]{0:T(128)S(1)}, f32[128]{0:T(128)}, u32[]{:S(2)}) copy-start(f32[128]{0:T(128)} %copy-done.95) | copy-start | bytes 1540
  351.5 203.6 %all-reduce.19.cloned.1.call-start = ((), (), s32[]{:S(2)}) async-start(), calls=%async_computation.7 | async-start | bytes 7667712 | tf_op jit(solution)/shard_map/psum | solution.py:285
  410.6 5.0 copy-start.104
  410.6 49.0 %copy-start.112 = (f32[128]{0:T(128)S(1)}, f32[128]{0:T(128)}, u32[]{:S(2)}) copy-start(f32[128]{0:T(128)} %copy-done.111) | copy-start | bytes 1540
  410.7 49.0 %copy-start.38 = (bf16[1,128,768]{2,1,0:T(8,128)(2,1)S(1)}, bf16[1,128,768]{2,1,0:T(8,128)(2,1)}, u32[]{:S(2)}) copy-start(bf16[1,128,768]{2,1,0:T(8,128)(2,1)} %param.24) | copy-start | bytes 589828
  (83 other events, 209.6 us)
Sparse Core Ops, SparseCore 0:
  104.6 61.9 all-gather.7
  168.2 22.6 all-gather.9
  199.0 60.1 all-gather.11
  262.2 31.4 reduce-scatter.4
  351.6 51.3 reduce-scatter.2
  407.2 147.8 all-reduce.18
